TPU v7x, 256 devices: a whole 4x4x8 slice. The times are simulated.
256 devices in a mesh: cell: 32 (over z, y_hi, core), period: 8 (over x, y_lo).
Axes of the slice: x: 4, y: 4 (y_hi: 2, y_lo: 2; y = y_hi * 2 + y_lo), z: 8, core: 2. Of those that a mesh axis runs over, the one named last changes fastest.
Arguments:
- footprints: float32 [32, 16, 32768], P(None, 'period', 'cell'), may hold values from -16 to 16
- cell_coords: int32 [2, 32768], P(None, 'cell'), may hold values from 0 to 255, as said below
- obs_period: int32 [32], replicated, may hold values from 0 to 15
- temporal_cov: float32 [16, 16], replicated, may hold values from -1.5 to 1.5
Outputs:
- hq_field: float32 [32, 16, 32768], P(None, 'period', 'cell')
- hqh_gram: float32 [32, 32], replicated
Inputs may be any that keep to these rules, and one draw needn't show every extreme that they name: `cell_coords`: cells sit at distinct grid points that together fill the rectangle of first coordinates 0 to 255 and second coordinates 0 to 127.
All inputs are finite; a program needn't handle non-finite values.
Results may differ from a plain program's by a relative error of at most 0.0003.
Values sent between devices are 32-bit elements; how exact they have to be, the bound alone decides.
No kernel may reach another device: no remote copies, remote signals or barrier semaphores. Data moves between devices by JAX's collectives and lax.ppermute only.
A program may use at most 64 MiB of HBM per device.

v0:
```python
import jax
import jax.numpy as jnp
from jax import lax
from jax.sharding import PartitionSpec as P

LENGTH_SCALE = 48.0
BLOCK_LIMIT = 4096


def covariance_tile(first_xy, second_xy):
    delta_x = first_xy[0][:, None] - second_xy[0][None, :]
    delta_y = first_xy[1][:, None] - second_xy[1][None, :]
    return jnp.exp(-jnp.sqrt(delta_x * delta_x + delta_y * delta_y) / LENGTH_SCALE)


def block_size(total_width, unit_width):
    unit_count = total_width // unit_width
    best_count = 1
    for factor in range(1, unit_count + 1):
        if unit_count % factor == 0 and factor * unit_width <= max(BLOCK_LIMIT, unit_width):
            best_count = factor
    return best_count * unit_width


def on_device(footprints, cell_coords, obs_period, temporal_cov):
    obs_count, per_local, cell_local = footprints.shape
    flat_count = obs_count * per_local
    period_first = lax.axis_index("period") * per_local
    period_ids = period_first + jnp.arange(per_local, dtype=jnp.int32)
    keep = (period_ids[None, :, None] <= obs_period[:, None, None]).astype(jnp.float32)
    masked = footprints * keep
    flat_rows = masked.reshape(flat_count, cell_local)
    local_places = cell_coords.astype(jnp.float32)
    empty = jnp.zeros((flat_count, cell_local), jnp.float32)
    piece_rows = lax.all_gather(flat_rows, "cell", axis=1, tiled=True)
    piece_places = lax.all_gather(local_places, "cell", axis=1, tiled=True)
    piece_width = piece_rows.shape[1]
    block_width = block_size(piece_width, cell_local)

    def add_block(block_index, running_sum):
        offset = block_index * block_width
        part_rows = lax.dynamic_slice_in_dim(piece_rows, offset, block_width, 1)
        part_places = lax.dynamic_slice_in_dim(piece_places, offset, block_width, 1)
        tile = covariance_tile(part_places, local_places)
        return running_sum + jnp.dot(
            part_rows, tile, precision=lax.Precision.HIGHEST, preferred_element_type=jnp.float32
        )

    spatial_flat = lax.fori_loop(0, piece_width // block_width, add_block, empty)
    spatial = spatial_flat.reshape(obs_count, per_local, cell_local)
    piece = lax.all_gather(spatial, "period", axis=1, tiled=True)
    weights = lax.dynamic_slice(temporal_cov, (period_first, 0), (per_local, piece.shape[1]))
    hq_field = jnp.einsum("tu,nuj->ntj", weights, piece, precision=lax.Precision.HIGHEST)
    partial_gram = jnp.einsum("ntj,mtj->nm", hq_field, masked, precision=lax.Precision.HIGHEST)
    hqh_gram = lax.psum(partial_gram, ("cell", "period"))
    return (hq_field, hqh_gram)


def solution(mesh):
    return jax.shard_map(
        on_device,
        mesh=mesh,
        in_specs=(P(None, "period", "cell"), P(None, "cell"), P(), P()),
        out_specs=(P(None, "period", "cell"), P()),
        check_vma=False,
    )
```

profile of v0, /device:TPU:1, one launch (start us, length us, event | category | flops | bytes accessed | tf_op | source)
XLA Modules:
  0.0 412.7 jit_solution(13719887616135554057)
XLA Ops:
  7.2 0.7 compare_convert_fusion
  8.1 1.1 broadcast_multiply_fusion
  9.2 0.9 reshape.51
  10.1 0.7 convert_element_type.12
  10.8 47.3 %all_gather.10 = f32[2,32768]{1,0:T(2,128)S(1)} all-gather(f32[2,1024]{1,0:T(2,128)S(1)} %convert_element_type.12), channel_id=1, replica_groups=mesh['cell'=32,'period'=8] {'cell'}, dimensions={1}, use_global_device_ids=true | all-gather | bytes 270336 | tf_op jit(solution)/shard_map/all_gather | solution.py:36
  58.1 58.6 %all-gather.3.cloned.1.call-done = f32[64,32768]{1,0:T(8,128)} async-done(((f32[64,1024]{1,0:T(8,128)}), f32[64,32768]{1,0:T(8,128)}) %all-gather.3.cloned.1.call-update) | async-done | bytes 8388624 | tf_op jit(solution)/shard_map/all_gather | solution.py:35
  116.7 157.3 %while.14 = (s32[]{:T(128)}, f32[64,1024]{1,0:T(8,128)S(1)}, f32[64,32768]{1,0:T(8,128)}, f32[2,32768]{1,0:T(2,128)S(1)}, f32[2,1024]{1,0:T(2,128)S(1)}, /*index...) while((s32[]{:T(128)}, f32[64,1024]{1,0:T(8,128)S(1)}, f32[64,32768]{1,0:T(8,128)}, ...), condition=%wide.region_1.0_spmd.clone, body=%wide.region_0.0_spmd.clone.sunk | while | flops 3250716672 | bytes 1695933 | solution.py:49
  116.8 19.5 %fusion.39 = f32[64,1024]{1,0:T(8,128)S(1)} fusion(f32[1024]{0:T(1024)S(1)} %bitcast.22, f32[4096]{0:T(1024)S(1)} %bitcast.20, f32[1024]{0:T(1024)S(1)} %bitcast.21, f32[4096]{0:T(1024)S(1)} %bitcast.19, f32[64,32768]{1,0:T(8,128)} %get-tuple-element.190, s32[]{:T(128)S(6)} %select_n.14, f32[64,1024]{1,0:T(8,128)S(1)} %get-tuple-element.179, ...), kind=kOutput, calls=%fused_computation.15.clone.1 | convolution fusion | flops 3250716672 | bytes 1613829 | tf_op jit(solution)/shard_map/while/body/eval_jaxpr/dot_general | solution.py:45
  136.3 0.1 constant_dynamic-slice_fusion.2
  136.4 19.5 %fusion.39 = f32[64,1024]{1,0:T(8,128)S(1)} fusion(f32[1024]{0:T(1024)S(1)} %bitcast.22, f32[4096]{0:T(1024)S(1)} %bitcast.20, f32[1024]{0:T(1024)S(1)} %bitcast.21, f32[4096]{0:T(1024)S(1)} %bitcast.19, f32[64,32768]{1,0:T(8,128)} %get-tuple-element.190, s32[]{:T(128)S(6)} %select_n.14, f32[64,1024]{1,0:T(8,128)S(1)} %get-tuple-element.179, ...), kind=kOutput, calls=%fused_computation.15.clone.1 | convolution fusion | flops 3250716672 | bytes 1613829 | tf_op jit(solution)/shard_map/while/body/eval_jaxpr/dot_general | solution.py:45
  156.0 0.1 constant_dynamic-slice_fusion.2
  156.1 19.5 %fusion.39 = f32[64,1024]{1,0:T(8,128)S(1)} fusion(f32[1024]{0:T(1024)S(1)} %bitcast.22, f32[4096]{0:T(1024)S(1)} %bitcast.20, f32[1024]{0:T(1024)S(1)} %bitcast.21, f32[4096]{0:T(1024)S(1)} %bitcast.19, f32[64,32768]{1,0:T(8,128)} %get-tuple-element.190, s32[]{:T(128)S(6)} %select_n.14, f32[64,1024]{1,0:T(8,128)S(1)} %get-tuple-element.179, ...), kind=kOutput, calls=%fused_computation.15.clone.1 | convolution fusion | flops 3250716672 | bytes 1613829 | tf_op jit(solution)/shard_map/while/body/eval_jaxpr/dot_general | solution.py:45
  175.6 0.1 constant_dynamic-slice_fusion.2
  175.7 19.5 %fusion.39 = f32[64,1024]{1,0:T(8,128)S(1)} fusion(f32[1024]{0:T(1024)S(1)} %bitcast.22, f32[4096]{0:T(1024)S(1)} %bitcast.20, f32[1024]{0:T(1024)S(1)} %bitcast.21, f32[4096]{0:T(1024)S(1)} %bitcast.19, f32[64,32768]{1,0:T(8,128)} %get-tuple-element.190, s32[]{:T(128)S(6)} %select_n.14, f32[64,1024]{1,0:T(8,128)S(1)} %get-tuple-element.179, ...), kind=kOutput, calls=%fused_computation.15.clone.1 | convolution fusion | flops 3250716672 | bytes 1613829 | tf_op jit(solution)/shard_map/while/body/eval_jaxpr/dot_general | solution.py:45
  195.4 19.5 %fusion.39 = f32[64,1024]{1,0:T(8,128)S(1)} fusion(f32[1024]{0:T(1024)S(1)} %bitcast.22, f32[4096]{0:T(1024)S(1)} %bitcast.20, f32[1024]{0:T(1024)S(1)} %bitcast.21, f32[4096]{0:T(1024)S(1)} %bitcast.19, f32[64,32768]{1,0:T(8,128)} %get-tuple-element.190, s32[]{:T(128)S(6)} %select_n.14, f32[64,1024]{1,0:T(8,128)S(1)} %get-tuple-element.179, ...), kind=kOutput, calls=%fused_computation.15.clone.1 | convolution fusion | flops 3250716672 | bytes 1613829 | tf_op jit(solution)/shard_map/while/body/eval_jaxpr/dot_general | solution.py:45
  215.0 19.5 %fusion.39 = f32[64,1024]{1,0:T(8,128)S(1)} fusion(f32[1024]{0:T(1024)S(1)} %bitcast.22, f32[4096]{0:T(1024)S(1)} %bitcast.20, f32[1024]{0:T(1024)S(1)} %bitcast.21, f32[4096]{0:T(1024)S(1)} %bitcast.19, f32[64,32768]{1,0:T(8,128)} %get-tuple-element.190, s32[]{:T(128)S(6)} %select_n.14, f32[64,1024]{1,0:T(8,128)S(1)} %get-tuple-element.179, ...), kind=kOutput, calls=%fused_computation.15.clone.1 | convolution fusion | flops 3250716672 | bytes 1613829 | tf_op jit(solution)/shard_map/while/body/eval_jaxpr/dot_general | solution.py:45
  234.7 19.5 %fusion.39 = f32[64,1024]{1,0:T(8,128)S(1)} fusion(f32[1024]{0:T(1024)S(1)} %bitcast.22, f32[4096]{0:T(1024)S(1)} %bitcast.20, f32[1024]{0:T(1024)S(1)} %bitcast.21, f32[4096]{0:T(1024)S(1)} %bitcast.19, f32[64,32768]{1,0:T(8,128)} %get-tuple-element.190, s32[]{:T(128)S(6)} %select_n.14, f32[64,1024]{1,0:T(8,128)S(1)} %get-tuple-element.179, ...), kind=kOutput, calls=%fused_computation.15.clone.1 | convolution fusion | flops 3250716672 | bytes 1613829 | tf_op jit(solution)/shard_map/while/body/eval_jaxpr/dot_general | solution.py:45
  254.3 19.5 %fusion.39 = f32[64,1024]{1,0:T(8,128)S(1)} fusion(f32[1024]{0:T(1024)S(1)} %bitcast.22, f32[4096]{0:T(1024)S(1)} %bitcast.20, f32[1024]{0:T(1024)S(1)} %bitcast.21, f32[4096]{0:T(1024)S(1)} %bitcast.19, f32[64,32768]{1,0:T(8,128)} %get-tuple-element.190, s32[]{:T(128)S(6)} %select_n.14, f32[64,1024]{1,0:T(8,128)S(1)} %get-tuple-element.179, ...), kind=kOutput, calls=%fused_computation.15.clone.1 | convolution fusion | flops 3250716672 | bytes 1613829 | tf_op jit(solution)/shard_map/while/body/eval_jaxpr/dot_general | solution.py:45
  274.0 0.1 reshape.52
  274.2 0.8 copy.16
  275.0 48.4 %all-gather.5.cloned.1.call-done = f32[32,16,1024]{2,0,1:T(8,128)} async-done(((f32[32,2,1024]{2,0,1:T(8,128)}), f32[32,16,1024]{2,0,1:T(8,128)}) %all-gather.5.cloned.1.call-update) | async-done | bytes 2097168 | tf_op jit(solution)/shard_map/all_gather | solution.py:51
  323.4 3.9 fusion.23
  327.3 0.5 convolution_bitcast_fusion
  327.7 78.1 %psum.7 = f32[32,32]{1,0:T(8,128)} all-reduce(f32[32,32]{1,0:T(8,128)S(1)} %convolution_bitcast_fusion), channel_id=1, replica_groups=mesh['cell'=32,'period'=8] {'cell','period'}, use_global_device_ids=true, to_apply=%region_2.0 | all-reduce | flops 1024 | bytes 8192 | tf_op jit(solution)/shard_map/psum | solution.py:55
  (24 shorter events, 0.8 us)
Async XLA Ops:
  7.2 316.2 %copy-start = (f32[16,16]{1,0:T(8,128)S(1)}, f32[16,16]{1,0:T(8,128)}, u32[]{:S(2)}) copy-start(f32[16,16]{1,0:T(8,128)} %param.9) | copy-start | bytes 3076
  7.2 109.5 %all-gather.3.cloned.1.call-start = ((), (), s32[]{:S(2)}) async-start(), calls=%async_computation | async-start | bytes 8650752 | tf_op jit(solution)/shard_map/all_gather | solution.py:35
  10.1 313.3 %all-gather.5.cloned.1.call-start = ((), (), s32[]{:S(2)}) async-start(), calls=%async_computation.1 | async-start | bytes 2359296 | tf_op jit(solution)/shard_map/all_gather | solution.py:51
  327.3 78.6 %copy-start.1 = (f32[32,2,1024]{2,1,0:T(2,128)}, f32[32,2,1024]{2,1,0:T(2,128)S(1)}, u32[]{:S(2)}) copy-start(f32[32,2,1024]{2,1,0:T(2,128)S(1)} %fusion.23) | copy-start | bytes 786436
Sparse Core Ops, SparseCore 0:
  11.4 105.2 all-gather.2
  275.1 48.2 all-gather.4
where the time goes:
time: 413 us
  matrix products  160 us (39%)
  blocking collectives  125 us (30%)
  waiting for transfers between devices  107 us (26%)
  between operations  14.1 us (3%)
    dot_general x8, matrix products, add_block(): jnp.dot(part_rows, tile, precision=lax.Precision.HIGHEST, preferred_eleme...  156 us
    psum x1, blocking collectives, on_device(): hqh_gram = lax.psum(partial_gram, ('cell', 'period'))  78.1 us
    all_gather x1, waiting for transfers between devices, on_device(): piece_rows = lax.all_gather(flat_rows, 'cell', axis=1, tiled=True)  58.6 us
    all_gather x1, waiting for transfers between devices, on_device(): piece = lax.all_gather(spatial, 'period', axis=1, tiled=True)  48.4 us
    all_gather x1, blocking collectives, on_device(): piece_places = lax.all_gather(local_places, 'cell', axis=1, tiled=True)  47.3 us
  transfers between devices with their start and end apart: 2, of which 2 were waited for; matrix products, arithmetic and copies ran while one was open for 0% of the time, Pallas kernels for 0%

commit v1 on v0

--- a/solution.py
+++ b/solution.py
@@ -52,7 +52,8 @@
     weights = lax.dynamic_slice(temporal_cov, (period_first, 0), (per_local, piece.shape[1]))
     hq_field = jnp.einsum("tu,nuj->ntj", weights, piece, precision=lax.Precision.HIGHEST)
     partial_gram = jnp.einsum("ntj,mtj->nm", hq_field, masked, precision=lax.Precision.HIGHEST)
-    hqh_gram = lax.psum(partial_gram, ("cell", "period"))
+    half = lax.psum(partial_gram, "period")
+    hqh_gram = lax.psum(half, "cell")
     return (hq_field, hqh_gram)
 
 

time: 413 us -> 496 us (1.20)
  blocking collectives: 125 us -> 205 us
    psum x1 -> x2, blocking collectives: 78.1 us -> 158 us  [the longest x1 131 us: on_device(): hqh_gram = lax.psum(half, 'cell')]
where the time goes in v1:
time: 496 us; the launch traced here: 492 us
  blocking collectives  205 us (41%)
  matrix products  160 us (32%)
  waiting for transfers between devices  107 us (22%)
  between operations  14.1 us (3%)
    dot_general x8, matrix products, add_block(): jnp.dot(part_rows, tile, precision=lax.Precision.HIGHEST, preferred_eleme...  156 us
    psum x1, blocking collectives, on_device(): hqh_gram = lax.psum(half, 'cell')  131 us
    all_gather x1, waiting for transfers between devices, on_device(): piece_rows = lax.all_gather(flat_rows, 'cell', axis=1, tiled=True)  58.6 us
    all_gather x1, waiting for transfers between devices, on_device(): piece = lax.all_gather(spatial, 'period', axis=1, tiled=True)  48.4 us
    all_gather x1, blocking collectives, on_device(): piece_places = lax.all_gather(local_places, 'cell', axis=1, tiled=True)  47.3 us
    psum x1, blocking collectives, on_device(): half = lax.psum(partial_gram, 'period')  26.5 us
  transfers between devices with their start and end apart: 2, of which 2 were waited for; matrix products, arithmetic and copies ran while one was open for 0% of the time, Pallas kernels for 0%

profile of v1, /device:TPU:1, one launch (start us, length us, event | category | flops | bytes accessed | tf_op | source)
XLA Modules:
  0.0 492.4 jit_solution(5073723794767255577)
XLA Ops:
  7.2 0.7 compare_convert_fusion
  8.1 1.1 broadcast_multiply_fusion
  9.2 0.9 reshape.51
  10.1 0.7 convert_element_type.12
  10.8 47.3 %all_gather.10 = f32[2,32768]{1,0:T(2,128)S(1)} all-gather(f32[2,1024]{1,0:T(2,128)S(1)} %convert_element_type.12), channel_id=1, replica_groups=mesh['cell'=32,'period'=8] {'cell'}, dimensions={1}, use_global_device_ids=true | all-gather | bytes 270336 | tf_op jit(solution)/shard_map/all_gather | solution.py:36
  58.1 58.6 %all-gather.3.cloned.1.call-done = f32[64,32768]{1,0:T(8,128)} async-done(((f32[64,1024]{1,0:T(8,128)}), f32[64,32768]{1,0:T(8,128)}) %all-gather.3.cloned.1.call-update) | async-done | bytes 8388624 | tf_op jit(solution)/shard_map/all_gather | solution.py:35
  116.7 157.3 %while.14 = (s32[]{:T(128)}, f32[64,1024]{1,0:T(8,128)S(1)}, f32[64,32768]{1,0:T(8,128)}, f32[2,32768]{1,0:T(2,128)S(1)}, f32[2,1024]{1,0:T(2,128)S(1)}, /*index...) while((s32[]{:T(128)}, f32[64,1024]{1,0:T(8,128)S(1)}, f32[64,32768]{1,0:T(8,128)}, ...), condition=%wide.region_1.0_spmd.clone, body=%wide.region_0.0_spmd.clone.sunk | while | flops 3250716672 | bytes 1695933 | solution.py:49
  116.8 19.5 %fusion.39 = f32[64,1024]{1,0:T(8,128)S(1)} fusion(f32[1024]{0:T(1024)S(1)} %bitcast.22, f32[4096]{0:T(1024)S(1)} %bitcast.20, f32[1024]{0:T(1024)S(1)} %bitcast.21, f32[4096]{0:T(1024)S(1)} %bitcast.19, f32[64,32768]{1,0:T(8,128)} %get-tuple-element.190, s32[]{:T(128)S(6)} %select_n.14, f32[64,1024]{1,0:T(8,128)S(1)} %get-tuple-element.179, ...), kind=kOutput, calls=%fused_computation.15.clone.1 | convolution fusion | flops 3250716672 | bytes 1613829 | tf_op jit(solution)/shard_map/while/body/eval_jaxpr/dot_general | solution.py:45
  136.3 0.1 constant_dynamic-slice_fusion.2
  136.4 19.5 %fusion.39 = f32[64,1024]{1,0:T(8,128)S(1)} fusion(f32[1024]{0:T(1024)S(1)} %bitcast.22, f32[4096]{0:T(1024)S(1)} %bitcast.20, f32[1024]{0:T(1024)S(1)} %bitcast.21, f32[4096]{0:T(1024)S(1)} %bitcast.19, f32[64,32768]{1,0:T(8,128)} %get-tuple-element.190, s32[]{:T(128)S(6)} %select_n.14, f32[64,1024]{1,0:T(8,128)S(1)} %get-tuple-element.179, ...), kind=kOutput, calls=%fused_computation.15.clone.1 | convolution fusion | flops 3250716672 | bytes 1613829 | tf_op jit(solution)/shard_map/while/body/eval_jaxpr/dot_general | solution.py:45
  156.0 0.1 constant_dynamic-slice_fusion.2
  156.1 19.5 %fusion.39 = f32[64,1024]{1,0:T(8,128)S(1)} fusion(f32[1024]{0:T(1024)S(1)} %bitcast.22, f32[4096]{0:T(1024)S(1)} %bitcast.20, f32[1024]{0:T(1024)S(1)} %bitcast.21, f32[4096]{0:T(1024)S(1)} %bitcast.19, f32[64,32768]{1,0:T(8,128)} %get-tuple-element.190, s32[]{:T(128)S(6)} %select_n.14, f32[64,1024]{1,0:T(8,128)S(1)} %get-tuple-element.179, ...), kind=kOutput, calls=%fused_computation.15.clone.1 | convolution fusion | flops 3250716672 | bytes 1613829 | tf_op jit(solution)/shard_map/while/body/eval_jaxpr/dot_general | solution.py:45
  175.7 19.5 %fusion.39 = f32[64,1024]{1,0:T(8,128)S(1)} fusion(f32[1024]{0:T(1024)S(1)} %bitcast.22, f32[4096]{0:T(1024)S(1)} %bitcast.20, f32[1024]{0:T(1024)S(1)} %bitcast.21, f32[4096]{0:T(1024)S(1)} %bitcast.19, f32[64,32768]{1,0:T(8,128)} %get-tuple-element.190, s32[]{:T(128)S(6)} %select_n.14, f32[64,1024]{1,0:T(8,128)S(1)} %get-tuple-element.179, ...), kind=kOutput, calls=%fused_computation.15.clone.1 | convolution fusion | flops 3250716672 | bytes 1613829 | tf_op jit(solution)/shard_map/while/body/eval_jaxpr/dot_general | solution.py:45
  195.4 19.5 %fusion.39 = f32[64,1024]{1,0:T(8,128)S(1)} fusion(f32[1024]{0:T(1024)S(1)} %bitcast.22, f32[4096]{0:T(1024)S(1)} %bitcast.20, f32[1024]{0:T(1024)S(1)} %bitcast.21, f32[4096]{0:T(1024)S(1)} %bitcast.19, f32[64,32768]{1,0:T(8,128)} %get-tuple-element.190, s32[]{:T(128)S(6)} %select_n.14, f32[64,1024]{1,0:T(8,128)S(1)} %get-tuple-element.179, ...), kind=kOutput, calls=%fused_computation.15.clone.1 | convolution fusion | flops 3250716672 | bytes 1613829 | tf_op jit(solution)/shard_map/while/body/eval_jaxpr/dot_general | solution.py:45
  215.0 19.5 %fusion.39 = f32[64,1024]{1,0:T(8,128)S(1)} fusion(f32[1024]{0:T(1024)S(1)} %bitcast.22, f32[4096]{0:T(1024)S(1)} %bitcast.20, f32[1024]{0:T(1024)S(1)} %bitcast.21, f32[4096]{0:T(1024)S(1)} %bitcast.19, f32[64,32768]{1,0:T(8,128)} %get-tuple-element.190, s32[]{:T(128)S(6)} %select_n.14, f32[64,1024]{1,0:T(8,128)S(1)} %get-tuple-element.179, ...), kind=kOutput, calls=%fused_computation.15.clone.1 | convolution fusion | flops 3250716672 | bytes 1613829 | tf_op jit(solution)/shard_map/while/body/eval_jaxpr/dot_general | solution.py:45
  234.7 19.5 %fusion.39 = f32[64,1024]{1,0:T(8,128)S(1)} fusion(f32[1024]{0:T(1024)S(1)} %bitcast.22, f32[4096]{0:T(1024)S(1)} %bitcast.20, f32[1024]{0:T(1024)S(1)} %bitcast.21, f32[4096]{0:T(1024)S(1)} %bitcast.19, f32[64,32768]{1,0:T(8,128)} %get-tuple-element.190, s32[]{:T(128)S(6)} %select_n.14, f32[64,1024]{1,0:T(8,128)S(1)} %get-tuple-element.179, ...), kind=kOutput, calls=%fused_computation.15.clone.1 | convolution fusion | flops 3250716672 | bytes 1613829 | tf_op jit(solution)/shard_map/while/body/eval_jaxpr/dot_general | solution.py:45
  254.3 19.5 %fusion.39 = f32[64,1024]{1,0:T(8,128)S(1)} fusion(f32[1024]{0:T(1024)S(1)} %bitcast.22, f32[4096]{0:T(1024)S(1)} %bitcast.20, f32[1024]{0:T(1024)S(1)} %bitcast.21, f32[4096]{0:T(1024)S(1)} %bitcast.19, f32[64,32768]{1,0:T(8,128)} %get-tuple-element.190, s32[]{:T(128)S(6)} %select_n.14, f32[64,1024]{1,0:T(8,128)S(1)} %get-tuple-element.179, ...), kind=kOutput, calls=%fused_computation.15.clone.1 | convolution fusion | flops 3250716672 | bytes 1613829 | tf_op jit(solution)/shard_map/while/body/eval_jaxpr/dot_general | solution.py:45
  274.0 0.1 reshape.52
  274.2 0.8 copy.16
  275.0 48.4 %all-gather.5.cloned.1.call-done = f32[32,16,1024]{2,0,1:T(8,128)} async-done(((f32[32,2,1024]{2,0,1:T(8,128)}), f32[32,16,1024]{2,0,1:T(8,128)}) %all-gather.5.cloned.1.call-update) | async-done | bytes 2097168 | tf_op jit(solution)/shard_map/all_gather | solution.py:51
  323.4 3.9 fusion.23
  327.3 0.5 convolution_bitcast_fusion
  327.7 26.5 %psum.14 = f32[32,32]{1,0:T(8,128)S(1)} all-reduce(f32[32,32]{1,0:T(8,128)S(1)} %convolution_bitcast_fusion), channel_id=1, replica_groups=mesh['cell'=32,'period'=8] {'period'}, use_global_device_ids=true, to_apply=%region_2.0 | all-reduce | flops 1024 | bytes 8192 | tf_op jit(solution)/shard_map/psum | solution.py:55
  354.2 131.3 %psum.15 = f32[32,32]{1,0:T(8,128)} all-reduce(f32[32,32]{1,0:T(8,128)S(1)} %psum.14), channel_id=1, replica_groups=mesh['cell'=32,'period'=8] {'cell'}, use_global_device_ids=true, to_apply=%region_3.0 | all-reduce | flops 1024 | bytes 8192 | tf_op jit(solution)/shard_map/psum | solution.py:56
  (25 shorter events, 0.9 us)
Async XLA Ops:
  7.2 316.2 %copy-start = (f32[16,16]{1,0:T(8,128)S(1)}, f32[16,16]{1,0:T(8,128)}, u32[]{:S(2)}) copy-start(f32[16,16]{1,0:T(8,128)} %param.9) | copy-start | bytes 3076
  7.2 109.5 %all-gather.3.cloned.1.call-start = ((), (), s32[]{:S(2)}) async-start(), calls=%async_computation | async-start | bytes 8650752 | tf_op jit(solution)/shard_map/all_gather | solution.py:35
  10.1 313.3 %all-gather.5.cloned.1.call-start = ((), (), s32[]{:S(2)}) async-start(), calls=%async_computation.1 | async-start | bytes 2359296 | tf_op jit(solution)/shard_map/all_gather | solution.py:51
  327.3 158.3 %copy-start.1 = (f32[32,2,1024]{2,1,0:T(2,128)}, f32[32,2,1024]{2,1,0:T(2,128)S(1)}, u32[]{:S(2)}) copy-start(f32[32,2,1024]{2,1,0:T(2,128)S(1)} %fusion.23) | copy-start | bytes 786436
Sparse Core Ops, SparseCore 0:
  11.4 105.2 all-gather.2
  275.1 48.2 all-gather.4
